TPU v7x, 32 devices: a whole 2x2x4 slice. The times are simulated.
32 devices in a mesh: dp: 8 (over z, x), tensor: 4 (over y, core).
Axes of the slice: x: 2, y: 2, z: 4, core: 2. Of those that a mesh axis runs over, the one named last changes fastest.
Arguments:
- tokens: bfloat16 [8192, 1024], P(('dp', 'tensor')), may hold values from -6 to 6
- segments: int32 [8, 1024], P('dp'), may hold values from 0 to 3, never falling along the last dimension, each value on 1 to 512 neighbouring positions
- cotangent: bfloat16 [8192, 1024], P(('dp', 'tensor')), may hold values from -6 to 6
- project_weight: bfloat16 [1024, 3, 1024], P('dp', None, 'tensor'), may hold values from -0.1875 to 0.1875
- output_weight: bfloat16 [1024, 1024], P('tensor', 'dp'), may hold values from -1.5 to 1.5
- up_weight: bfloat16 [1024, 4096], P('dp', 'tensor'), may hold values from -0.1875 to 0.1875
- down_weight: bfloat16 [4096, 1024], P('tensor', 'dp'), may hold values from -0.09375 to 0.09375
- norm_gains: float32 [2, 1024], replicated, may hold values from 0.5 to 1.5
- bias_rows: float32 [6, 1024], replicated, may hold values from -3 to 3
- hidden_bias: float32 [4096], replicated, may hold values from -3 to 3
Outputs:
- layer_out: bfloat16 [8192, 1024], P(('dp', 'tensor'))
- grad_tokens: float32 [8192, 1024], P(('dp', 'tensor'))
- grad_project: float32 [1024, 3, 1024], P('dp', None, 'tensor')
- grad_output: float32 [1024, 1024], P('tensor', 'dp')
- grad_up: float32 [1024, 4096], P('dp', 'tensor')
- grad_down: float32 [4096, 1024], P('tensor', 'dp')
- grad_gains: float32 [2, 1024], replicated
- grad_bias_rows: float32 [6, 1024], replicated
- grad_hidden_bias: float32 [4096], replicated
Inputs may be any that keep to these rules, and one draw needn't show every extreme that they name: `segments`: within each sequence the numbers never fall; a document is a run of equal numbers of at most 512 tokens, and every sequence has one document of exactly that length.
All inputs are finite; a program needn't handle non-finite values.
Results may differ from a plain program's by a relative error of at most 0.015.
The roundings to bfloat16 on the way count: a program that leaves them out, or rounds other values in their place, can miss the bound.
Values may be sent and summed in bfloat16 or wider, within the bound.
A program may use at most 128 MiB of HBM per device.

v0:
```python
import jax
import jax.numpy as jnp
from jax import lax
from jax.sharding import PartitionSpec as P

HEAD = 64
EPSILON = 1e-05
NEGATIVE = -1e30


def gelu_exact(values):
    return jax.nn.gelu(values, approximate=False)


def layer_norm(token_rows, gain, shift):
    average = jnp.mean(token_rows, axis=-1, keepdims=True)
    centred = token_rows - average
    variance = jnp.mean(centred * centred, axis=-1, keepdims=True)
    inverse = lax.rsqrt(variance + EPSILON)
    normed = centred * inverse
    return (normed * gain + shift, (normed, inverse))


def norm_back(grad_rows, saved, gain):
    normed, inverse = saved
    grad_gain = jnp.sum(grad_rows * normed, axis=0)
    grad_shift = jnp.sum(grad_rows, axis=0)
    grad_normed = grad_rows * gain
    grad_input = inverse * (
        grad_normed
        - jnp.mean(grad_normed, axis=-1, keepdims=True)
        - normed * jnp.mean(grad_normed * normed, axis=-1, keepdims=True)
    )
    return (grad_input, grad_gain, grad_shift)


def split_heads(token_rows):
    return token_rows.reshape(token_rows.shape[0], token_rows.shape[1] // HEAD, HEAD)


def scatter_sum(partial_sum, axis_name, dimension):
    return lax.psum_scatter(
        partial_sum.astype(jnp.bfloat16), axis_name, scatter_dimension=dimension, tiled=True
    ).astype(jnp.float32)


def place_columns(partial_sum, column_block, total_width):
    full_rows = jnp.zeros(partial_sum.shape[:-1] + (total_width,), jnp.float32)
    return lax.dynamic_update_slice_in_dim(
        full_rows, partial_sum, column_block * partial_sum.shape[-1], partial_sum.ndim - 1
    )


def per_device(
    tokens,
    segments,
    cotangent,
    project_weight,
    output_weight,
    up_weight,
    down_weight,
    norm_gains,
    bias_rows,
    hidden_bias,
):
    tensor_rank = lax.axis_index("tensor")
    local_rows, model_width = tokens.shape
    seq_count, seq_length = segments.shape
    group_rows = seq_count * seq_length
    local_width = project_weight.shape[2]
    score_scale = HEAD ** (-0.5)
    block_rows = min(512, seq_length)
    per_sequence = seq_length // block_rows
    count_blocks = group_rows // block_rows
    block_ids = jnp.arange(count_blocks, dtype=jnp.int32)
    triple_full, output_full, upward_full, downward_full = (
        lax.all_gather(project_weight, "dp", axis=0, tiled=True),
        lax.all_gather(output_weight, "dp", axis=1, tiled=True),
        lax.all_gather(up_weight, "dp", axis=0, tiled=True),
        lax.all_gather(down_weight, "dp", axis=1, tiled=True),
    )
    local_hidden = upward_full.shape[1]
    triple_matrix = triple_full.reshape(model_width, 3 * local_width)
    gathered = lax.all_gather(tokens, "tensor", axis=0, tiled=True)
    head_bias = lax.dynamic_slice_in_dim(bias_rows, tensor_rank * local_width, local_width, 1)
    projected = jnp.dot(gathered, triple_matrix, preferred_element_type=jnp.float32).reshape(
        group_rows, 3, local_width
    )
    queries = (projected[:, 0] + head_bias[0]).astype(jnp.bfloat16)
    key_rows = projected[:, 1].astype(jnp.bfloat16)
    value_rows = (projected[:, 2] + head_bias[1]).astype(jnp.bfloat16)

    def block_parts(block_index):
        sequence = block_index // per_sequence
        row_start = block_index * block_rows
        seq_start = sequence * seq_length
        query_block = split_heads(lax.dynamic_slice_in_dim(queries, row_start, block_rows, 0))
        key_block = split_heads(key_rows)
        value_block = split_heads(value_rows)
        seq_ids = lax.dynamic_index_in_dim(segments, sequence, 0, keepdims=False)
        query_ids = lax.dynamic_slice_in_dim(seq_ids, row_start - seq_start, block_rows, 0)
        products = (
            jnp.einsum("qhd,khd->hqk", query_block, key_block, preferred_element_type=jnp.float32)
            * score_scale
        )
        scores = jnp.where((query_ids[:, None] == seq_ids[None, :])[None], products, NEGATIVE)
        return (row_start, query_block, key_block, value_block, scores)

    def forward_block(block_index):
        row_start, query_block, key_block, value_block, scores = block_parts(block_index)
        row_max = jnp.max(scores, axis=-1, keepdims=True)
        exponent = jnp.exp(scores - row_max)
        row_sum = jnp.sum(exponent, axis=-1, keepdims=True)
        weights_low = (exponent / row_sum).astype(jnp.bfloat16)
        mixed_block = jnp.einsum(
            "hqk,khd->qhd", weights_low, value_block, preferred_element_type=jnp.float32
        )
        log_total = row_max[:, :, 0] + jnp.log(row_sum[:, :, 0])
        return (mixed_block.reshape(block_rows, local_width).astype(jnp.bfloat16), log_total)

    mixed_blocks, log_totals = lax.map(forward_block, block_ids)
    mixed_rows = mixed_blocks.reshape(group_rows, local_width)
    branch_out = (
        scatter_sum(
            jnp.dot(mixed_rows, output_full, preferred_element_type=jnp.float32), "tensor", 0
        )
        + bias_rows[2]
    )
    first_out, first_saved = layer_norm(
        tokens.astype(jnp.float32) + branch_out, norm_gains[0], bias_rows[3]
    )
    first_gathered = lax.all_gather(first_out.astype(jnp.bfloat16), "tensor", axis=0, tiled=True)
    local_bias = lax.dynamic_slice_in_dim(hidden_bias, tensor_rank * local_hidden, local_hidden, 0)
    upper_rows = (
        jnp.dot(first_gathered, upward_full, preferred_element_type=jnp.float32) + local_bias
    )
    hidden_full, gelu_back = jax.vjp(gelu_exact, upper_rows)
    hidden_rows = hidden_full.astype(jnp.bfloat16)
    second_out = (
        scatter_sum(
            jnp.dot(hidden_rows, downward_full, preferred_element_type=jnp.float32), "tensor", 0
        )
        + bias_rows[4]
    )
    layer_out, second_saved = layer_norm(first_out + second_out, norm_gains[1], bias_rows[5])
    reloaded = (
        lax.all_gather(project_weight, "dp", axis=0, tiled=True),
        lax.all_gather(output_weight, "dp", axis=1, tiled=True),
        lax.all_gather(up_weight, "dp", axis=0, tiled=True),
        lax.all_gather(down_weight, "dp", axis=1, tiled=True),
    )
    back_triple = reloaded[0].reshape(model_width, 3 * local_width)
    back_output, back_upward, back_downward = (reloaded[1], reloaded[2], reloaded[3])
    grad_layer = cotangent.astype(jnp.float32)
    grad_second_in, grad_gain_two, grad_shift_two = norm_back(
        grad_layer, second_saved, norm_gains[1]
    )
    grad_second = grad_second_in.astype(jnp.bfloat16)
    grad_second_all = lax.all_gather(grad_second, "tensor", axis=0, tiled=True)
    grad_down_part = jnp.einsum(
        "tf,td->fd", hidden_rows, grad_second_all, preferred_element_type=jnp.float32
    )
    grad_hidden = jnp.einsum(
        "td,fd->tf", grad_second_all, back_downward, preferred_element_type=jnp.float32
    )
    grad_upper = gelu_back(grad_hidden)[0].astype(jnp.bfloat16)
    grad_up_part = jnp.einsum(
        "td,tf->df", first_gathered, grad_upper, preferred_element_type=jnp.float32
    )
    grad_first = (
        scatter_sum(
            jnp.einsum("tf,df->td", grad_upper, back_upward, preferred_element_type=jnp.float32),
            "tensor",
            0,
        )
        + grad_second_in
    )
    grad_first_in, grad_gain_one, grad_shift_one = norm_back(grad_first, first_saved, norm_gains[0])
    grad_branch = grad_first_in.astype(jnp.bfloat16)
    grad_branch_all = lax.all_gather(grad_branch, "tensor", axis=0, tiled=True)
    grad_output_part = jnp.einsum(
        "tc,td->cd", mixed_rows, grad_branch_all, preferred_element_type=jnp.float32
    )
    grad_mixed = jnp.einsum(
        "td,cd->tc", grad_branch_all, back_output, preferred_element_type=jnp.float32
    ).astype(jnp.bfloat16)

    def backward_block(block_index):
        row_start, query_block, key_block, value_block, scores = block_parts(block_index)
        weights_full = jnp.exp(scores - log_totals[block_index][:, :, None])
        grad_mixed_block = split_heads(
            lax.dynamic_slice_in_dim(grad_mixed, row_start, block_rows, 0)
        )
        grad_weights = jnp.einsum(
            "qhd,khd->hqk", grad_mixed_block, value_block, preferred_element_type=jnp.float32
        )
        row_dot = jnp.sum(weights_full * grad_weights, axis=-1, keepdims=True)
        grad_scores = (weights_full * (grad_weights - row_dot)).astype(jnp.bfloat16)
        grad_query = (
            jnp.einsum("hqk,khd->qhd", grad_scores, key_block, preferred_element_type=jnp.float32)
            * score_scale
        )
        grad_key = (
            jnp.einsum("hqk,qhd->khd", grad_scores, query_block, preferred_element_type=jnp.float32)
            * score_scale
        )
        grad_value = jnp.einsum(
            "hqk,qhd->khd",
            weights_full.astype(jnp.bfloat16),
            grad_mixed_block,
            preferred_element_type=jnp.float32,
        )
        return (
            grad_query.reshape(block_rows, local_width),
            grad_key.reshape(seq_length, local_width),
            grad_value.reshape(seq_length, local_width),
        )

    query_blocks, key_blocks, value_blocks = lax.map(backward_block, block_ids)
    grad_queries = query_blocks.reshape(group_rows, local_width)
    grad_keys = (
        key_blocks.reshape(seq_count, per_sequence, seq_length, local_width)
        .sum(axis=1)
        .reshape(group_rows, local_width)
    )
    grad_values = (
        value_blocks.reshape(seq_count, per_sequence, seq_length, local_width)
        .sum(axis=1)
        .reshape(group_rows, local_width)
    )
    grad_projected = jnp.stack((grad_queries, grad_keys, grad_values), axis=1).astype(jnp.bfloat16)
    grad_project_part = jnp.einsum(
        "te,tsc->esc", gathered, grad_projected, preferred_element_type=jnp.float32
    )
    grad_matrix = grad_projected.reshape(group_rows, 3 * local_width)
    grad_tokens = (
        lax.psum_scatter(
            jnp.einsum(
                "tc,ec->te", grad_matrix, back_triple, preferred_element_type=jnp.float32
            ).astype(jnp.bfloat16),
            "tensor",
            scatter_dimension=0,
            tiled=True,
        ).astype(jnp.float32)
        + grad_first_in
    )
    grad_project, grad_output, grad_up, grad_down = (
        scatter_sum(grad_project_part, "dp", 0),
        scatter_sum(grad_output_part, "dp", 1),
        scatter_sum(grad_up_part, "dp", 0),
        scatter_sum(grad_down_part, "dp", 1),
    )
    head_terms = place_columns(
        jnp.stack(
            (
                jnp.sum(grad_projected[:, 0], axis=0, dtype=jnp.float32),
                jnp.sum(grad_projected[:, 2], axis=0, dtype=jnp.float32),
            )
        ),
        tensor_rank,
        model_width,
    )
    shared_terms = jnp.stack(
        (
            jnp.sum(grad_branch, axis=0, dtype=jnp.float32),
            grad_shift_one,
            jnp.sum(grad_second, axis=0, dtype=jnp.float32),
            grad_shift_two,
        )
    )
    bias_terms = jnp.concatenate((head_terms, shared_terms), axis=0)
    gain_terms = jnp.stack((grad_gain_one, grad_gain_two))
    hidden_terms = place_columns(
        jnp.sum(grad_upper, axis=0, dtype=jnp.float32), tensor_rank, hidden_bias.shape[0]
    )
    grad_gains, grad_bias_rows, grad_hidden_bias = lax.psum(
        (gain_terms, bias_terms, hidden_terms), ("dp", "tensor")
    )
    return (
        layer_out.astype(jnp.bfloat16),
        grad_tokens,
        grad_project,
        grad_output,
        grad_up,
        grad_down,
        grad_gains,
        grad_bias_rows,
        grad_hidden_bias,
    )


def solution(mesh):
    placed = (
        P(("dp", "tensor"), None),
        P("dp", None),
        P(("dp", "tensor"), None),
        P("dp", None, "tensor"),
        P("tensor", "dp"),
        P("dp", "tensor"),
        P("tensor", "dp"),
        P(),
        P(),
        P(),
    )
    return jax.shard_map(
        per_device,
        mesh=mesh,
        in_specs=placed,
        out_specs=(
            P(("dp", "tensor"), None),
            P(("dp", "tensor"), None),
            P("dp", None, "tensor"),
            P("tensor", "dp"),
            P("dp", "tensor"),
            P("tensor", "dp"),
            P(),
            P(),
            P(),
        ),
        check_vma=False,
    )
```

profile of v0, /device:TPU:0, one launch (start us, length us, event | category | flops | bytes accessed | tf_op | source)
XLA Modules:
  0.0 727.4 jit_solution(16687060974636816753)
XLA Ops:
  9.6 31.2 %all_gather.30 = bf16[256,1024]{1,0:T(8,128)(2,1)S(1)} all-gather(bf16[256,128]{1,0:T(8,128)(2,1)} %param.18), channel_id=1, replica_groups=mesh['dp'=8,'tensor'=4] {'dp'}, dimensions={1}, use_global_device_ids=true | all-gather | bytes 589824 | tf_op jit(solution)/shard_map/all_gather | solution.py:78
  40.7 18.4 %all-gather.10.cloned.1.call-done = bf16[1024,3,256]{2,0,1:T(8,128)(2,1)} async-done(((bf16[128,3,256]{2,0,1:T(8,128)(2,1)}), bf16[1024,3,256]{2,0,1:T(8,128)(2,1)}) %all-gather.10.cloned.1.call-update) | async-done | bytes 1572880 | tf_op jit(solution)/shard_map/all_gather | solution.py:77
  60.8 21.3 %all-gather.8.cloned.1.call-done = bf16[1024,1024]{1,0:T(8,128)(2,1)} async-done(((bf16[256,1024]{1,0:T(8,128)(2,1)}), bf16[1024,1024]{1,0:T(8,128)(2,1)}) %all-gather.8.cloned.1.call-update) | async-done | bytes 2097168 | tf_op jit(solution)/shard_map/all_gather | solution.py:84
  82.1 3.4 fusion.20
  89.6 22.9 %while.30 = (s32[]{:T(128)}, bf16[2,512,256]{2,1,0:T(8,128)(2,1)S(1)}, f32[2,4,512]{2,1,0:T(4,128)S(1)}, s32[2]{0:T(128)S(1)}, s32[1,1024]{1,0:T(1,128)S(1)}, /*...) while((s32[]{:T(128)}, ...), condition=%wide.region_3.4_spmd, body=%wide.region_0.3_spmd.sunk | while | flops 562690048 | bytes 30484896 | solution.py:121
  95.6 2.3 fusion.103
  97.9 2.9 fusion.104
  107.0 2.3 fusion.103
  109.3 2.9 fusion.104
  112.5 2.0 convolution_convert_fusion.4
  115.2 30.9 %reduce-scatter.15.cloned.1.call-done = bf16[256,1024]{1,0:T(8,128)(2,1)} async-done(((bf16[1024,1024]{1,0:T(8,128)(2,1)}), bf16[256,1024]{1,0:T(8,128)(2,1)}) %reduce-scatter.15.cloned.1.call-update) | async-done | bytes 524304 | tf_op jit(solution)/shard_map/reduce_scatter | solution.py:42
  148.8 2.1 fusion.37
  152.8 44.8 %all-gather.14.cloned.1.call-done = bf16[1024,1024]{1,0:T(8,128)(2,1)} async-done(((bf16[128,1024]{1,0:T(8,128)(2,1)}), bf16[1024,1024]{1,0:T(8,128)(2,1)}) %all-gather.14.cloned.1.call-update) | async-done | bytes 2097168 | tf_op jit(solution)/shard_map/all_gather | solution.py:79
  197.7 23.2 %all-gather.12.cloned.1.call-done = bf16[1024,1024]{1,0:T(8,128)(2,1)} async-done(((bf16[256,1024]{1,0:T(8,128)(2,1)}), bf16[1024,1024]{1,0:T(8,128)(2,1)}) %all-gather.12.cloned.1.call-update) | async-done | bytes 2097168 | tf_op jit(solution)/shard_map/all_gather | solution.py:132
  220.8 14.9 %multiply_convert_fusion.1 = (bf16[1024,1024]{1,0:T(8,128)(2,1)}, f32[1024,1024]{1,0:T(8,128)}, f32[1024,1024]{1,0:T(8,128)}) fusion(f32[1024]{0:T(1024)S(1)} %dynamic_slice.57, bf16[1024,1024]{1,0:T(8,128)(2,1)} %all-gather.12.cloned.1.call-done, bf16[1024,1024]{1,0:T(8,128)(2,1)} %all-gather.14.cloned.1.call-done), kind=kOutput, calls=%fused_computation.37 | convolution fusion | flops 2216689664 | bytes 14684160 | tf_op jit(solution)/shard_map/dot_general | solution.py:135
  235.7 38.3 %all-gather.16.cloned.1.call-done = bf16[1024,1024]{1,0:T(8,128)(2,1)} async-done(((bf16[1024,128]{1,0:T(8,128)(2,1)}), bf16[1024,1024]{1,0:T(8,128)(2,1)}) %all-gather.16.cloned.1.call-update) | async-done | bytes 2097168 | tf_op jit(solution)/shard_map/all_gather | solution.py:80
  274.0 6.0 convolution_convert_fusion.3
  280.1 29.7 %reduce-scatter.17.cloned.1.call-done = bf16[256,1024]{1,0:T(8,128)(2,1)} async-done(((bf16[1024,1024]{1,0:T(8,128)(2,1)}), bf16[256,1024]{1,0:T(8,128)(2,1)}) %reduce-scatter.17.cloned.1.call-update) | async-done | bytes 524304 | tf_op jit(solution)/shard_map/reduce_scatter | solution.py:42
  312.7 2.4 convert_reduce_fusion.2
  315.4 22.5 %all-gather.18.cloned.1.call-done = bf16[1024,1024]{1,0:T(8,128)(2,1)} async-done(((bf16[256,1024]{1,0:T(8,128)(2,1)}), bf16[1024,1024]{1,0:T(8,128)(2,1)}) %all-gather.18.cloned.1.call-update) | async-done | bytes 2097168 | tf_op jit(solution)/shard_map/all_gather | solution.py:159
  337.9 8.5 %convert_reduce_fusion = (f32[1024]{0:T(1024)S(1)}, bf16[1024,1024]{1,0:T(8,128)(2,1)S(1)}) fusion(f32[1024,1024]{1,0:T(8,128)} %get-tuple-element.401, f32[1024,1024]{1,0:T(8,128)} %get-tuple-element.419, f32[1024]{0:T(1024)S(1)} %dynamic_slice.57, bf16[1024,1024]{1,0:T(8,128)(2,1)} %all-gather.18.cloned.1.call-done, ...), kind=kOutput, calls=%fused_computation.35 | convolution fusion | flops 2165308416 | bytes 14688256 | tf_op jit(solution)/shard_map/td,fd->tf/dot_general | solution.py:163
  347.7 3.7 convolution_convert_fusion.2
  351.5 31.6 %reduce-scatter.19.cloned.1.call-done = bf16[256,1024]{1,0:T(8,128)(2,1)} async-done(((bf16[1024,1024]{1,0:T(8,128)(2,1)}), bf16[256,1024]{1,0:T(8,128)(2,1)}) %reduce-scatter.19.cloned.1.call-update) | async-done | bytes 524304 | tf_op jit(solution)/shard_map/reduce_scatter | solution.py:42
  383.1 2.0 multiply_reduce_fusion.1
  385.1 3.0 convert_reduce_fusion.3
  388.2 5.9 convolution_convert_fusion
  394.1 4.1 copy.60
  398.3 6.0 convolution_convert_fusion.1
  404.5 6.4 all-gather.20.cloned.1.call-done
  410.9 2.3 convolution_convert_fusion.5
  414.3 2.3 convolution_convert_fusion.6
  416.7 42.4 %while.31 = (s32[]{:T(128)}, bf16[2,512,256]{1,2,0:T(8,128)(2,1)}, f32[2,1024,256]{1,2,0:T(8,128)}, f32[2,1024,256]{1,2,0:T(8,128)}, s32[2]{0:T(128)S(1)}, /*ind...) while((s32[]{:T(128)}, bf16[2,512,256]{1,2,0:T(8,128)(2,1)}, ...), condition=%wide.region_17.18_spmd, body=%wide.region_15.17_spmd.sunk | while | flops 1374681088 | bytes 114100872 | solution.py:219
  423.8 2.4 fusion.116
  426.2 3.2 multiply_reduce_fusion.7
  429.4 2.4 multiply_convert_fusion.3
  444.9 2.4 fusion.116
  447.3 3.2 multiply_reduce_fusion.7
  450.4 2.4 multiply_convert_fusion.3
  463.5 4.6 fusion.22
  468.1 2.6 copy.62
  470.8 4.6 bitcast_convert_fusion
  475.7 7.3 %reduce-scatter.29.cloned.1.call-done = bf16[128,1024]{1,0:T(8,128)(2,1)} async-done(((bf16[1024,1024]{1,0:T(8,128)(2,1)}), bf16[128,1024]{1,0:T(8,128)(2,1)}) %reduce-scatter.29.cloned.1.call-update) | async-done | bytes 262160
  485.0 68.5 %reduce-scatter.23.cloned.1.call-done = bf16[128,1024]{1,0:T(8,128)(2,1)} async-done(((bf16[1024,1024]{1,0:T(8,128)(2,1)}), bf16[128,1024]{1,0:T(8,128)(2,1)}) %reduce-scatter.23.cloned.1.call-update) | async-done | bytes 262160 | tf_op jit(solution)/shard_map/reduce_scatter | solution.py:42
  555.7 41.0 %all-reduce = (f32[2,1024]{1,0:T(2,128)}, f32[6,1024]{1,0:T(8,128)}, f32[4096]{0:T(1024)}) all-reduce(f32[2,1024]{1,0:T(2,128)S(1)} %pad_maximum_fusion.3, f32[6,1024]{1,0:T(8,128)S(1)} %concatenate.3, f32[4096]{0:T(1024)S(1)} %dynamic_update_slice.41), channel_id=1, replica_groups=mesh['dp'=8,'tensor'=4] {'dp','tensor'}, use_global_device_ids=true, to_apply=%region_27.28 | all-reduce | flops 12288 | bytes 98304 | tf_op jit(solution)/shard_map/psum | solution.py:276
  596.8 21.4 %reduce-scatter.27.cloned.1.call-done = bf16[128,256]{1,0:T(8,128)(2,1)} async-done(((bf16[1024,256]{1,0:T(8,128)(2,1)}), bf16[128,256]{1,0:T(8,128)(2,1)}) %reduce-scatter.27.cloned.1.call-update) | async-done | bytes 65552
  619.8 65.6 %reduce-scatter.25.cloned.1.call-done = bf16[128,768]{1,0:T(8,128)(2,1)} async-done(((bf16[1024,768]{1,0:T(8,128)(2,1)}), bf16[128,768]{1,0:T(8,128)(2,1)}) %reduce-scatter.25.cloned.1.call-update) | async-done | bytes 196624
  687.4 30.9 %reduce-scatter.21.cloned.1.call-done = bf16[256,1024]{1,0:T(8,128)(2,1)} async-done(((bf16[1024,1024]{1,0:T(8,128)(2,1)}), bf16[256,1024]{1,0:T(8,128)(2,1)}) %reduce-scatter.21.cloned.1.call-update) | async-done | bytes 524304 | tf_op jit(solution)/shard_map/reduce_scatter | solution.py:237
  718.3 2.2 convert_add_fusion
  (180 shorter events, 54.4 us)
Async XLA Ops:
  7.2 51.9 %all-gather.10.cloned.1.call-start = ((), (), s32[]{:S(2)}) async-start(), calls=%async_computation.9 | async-start | bytes 1769472 | tf_op jit(solution)/shard_map/all_gather | solution.py:77
  7.9 74.2 %all-gather.8.cloned.1.call-start = ((), (), s32[]{:S(2)}) async-start(), calls=%async_computation.8 | async-start | bytes 2621440 | tf_op jit(solution)/shard_map/all_gather | solution.py:84
  8.7 137.5 %reduce-scatter.15.cloned.1.call-start = ((), (), s32[]{:S(2)}) async-start(), calls=%async_computation.10 | async-start | bytes 2621440 | tf_op jit(solution)/shard_map/reduce_scatter | solution.py:42
  40.7 71.8 %copy-start.9 = (bf16[256,1024]{1,0:T(8,128)(2,1)}, bf16[256,1024]{1,0:T(8,128)(2,1)S(1)}, u32[]{:S(2)}) copy-start(bf16[256,1024]{1,0:T(8,128)(2,1)S(1)} %all_gather.30) | copy-start | bytes 1572868
  85.5 1.7 copy-start.3
  87.2 2.4 copy-start.13
  112.5 38.5 %copy-start.11 = (bf16[2,512,256]{2,1,0:T(8,128)(2,1)}, bf16[2,512,256]{2,1,0:T(8,128)(2,1)S(1)}, u32[]{:S(2)}) copy-start(bf16[2,512,256]{2,1,0:T(8,128)(2,1)S(1)} %get-tuple-element.252) | copy-start | bytes 1572868
  112.5 2.7 copy-start.21
  112.5 2.7 copy-start.20
  112.5 33.6 %copy-start = (bf16[256,1024]{1,0:T(8,128)(2,1)S(1)}, bf16[256,1024]{1,0:T(8,128)(2,1)}, u32[]{:S(2)}) copy-start(bf16[256,1024]{1,0:T(8,128)(2,1)} %param.14) | copy-start | bytes 1572868
  114.6 83.1 %all-gather.14.cloned.1.call-start = ((), (), s32[]{:S(2)}) async-start(), calls=%async_computation.12 | async-start | bytes 2359296 | tf_op jit(solution)/shard_map/all_gather | solution.py:79
  115.1 105.7 %all-gather.12.cloned.1.call-start = ((), (), s32[]{:S(2)}) async-start(), calls=%async_computation.11 | async-start | bytes 2621440 | tf_op jit(solution)/shard_map/all_gather | solution.py:132
  151.0 123.1 %all-gather.16.cloned.1.call-start = ((), (), s32[]{:S(2)}) async-start(), calls=%async_computation.13 | async-start | bytes 2359296 | tf_op jit(solution)/shard_map/all_gather | solution.py:80
  151.6 158.2 %reduce-scatter.17.cloned.1.call-start = ((), (), s32[]{:S(2)}) async-start(), calls=%async_computation.14 | async-start | bytes 2621440 | tf_op jit(solution)/shard_map/reduce_scatter | solution.py:42
  274.0 35.8 %copy-start.1 = (bf16[256,1024]{1,0:T(8,128)(2,1)S(1)}, bf16[256,1024]{1,0:T(8,128)(2,1)}, u32[]{:S(2)}) copy-start(bf16[256,1024]{1,0:T(8,128)(2,1)} %reduce-scatter.15.cloned.1.call-done) | copy-start | bytes 1572868
  280.0 31.6 %copy-start.4 = (bf16[256,1024]{1,0:T(8,128)(2,1)S(1)}, bf16[256,1024]{1,0:T(8,128)(2,1)}, u32[]{:S(2)}) copy-start(bf16[256,1024]{1,0:T(8,128)(2,1)} %param.16) | copy-start | bytes 1572868
  280.0 57.9 %all-gather.18.cloned.1.call-start = ((), (), s32[]{:S(2)}) async-start(), calls=%async_computation.15 | async-start | bytes 2621440 | tf_op jit(solution)/shard_map/all_gather | solution.py:159
  315.2 67.9 %reduce-scatter.19.cloned.1.call-start = ((), (), s32[]{:S(2)}) async-start(), calls=%async_computation.16 | async-start | bytes 2621440 | tf_op jit(solution)/shard_map/reduce_scatter | solution.py:42
  337.9 9.8 %copy-start.22 = (bf16[1024,1024]{1,0:T(8,128)(2,1)S(1)}, bf16[1024,1024]{1,0:T(8,128)(2,1)}, u32[]{:S(2)}) copy-start(bf16[1024,1024]{1,0:T(8,128)(2,1)} %all-gather.14.cloned.1.call-done) | copy-start | bytes 6291460
  346.4 1.3 copy-start.23
  351.5 59.4 %all-gather.20.cloned.1.call-start = ((), (), s32[]{:S(2)}) async-start(), calls=%async_computation.17 | async-start | bytes 2621440 | tf_op jit(solution)/shard_map/all_gather | solution.py:180
  388.2 94.9 %reduce-scatter.29.cloned.1.call-start = ((), (), s32[]{:S(2)}) async-start(), calls=%async_computation.22 | async-start | bytes 2359296
  398.2 12.7 %copy-start.12 = (bf16[2,512,256]{2,1,0:T(8,128)(2,1)S(1)}, bf16[2,512,256]{2,1,0:T(8,128)(2,1)}, u32[]{:S(2)}) copy-start(bf16[2,512,256]{2,1,0:T(8,128)(2,1)} %copy-done.11) | copy-start | bytes 1572868
  398.2 155.3 %reduce-scatter.23.cloned.1.call-start = ((), (), s32[]{:S(2)}) async-start(), calls=%async_computation.19 | async-start | bytes 2359296 | tf_op jit(solution)/shard_map/reduce_scatter | solution.py:42
  404.2 10.1 %copy-start.10 = (bf16[256,1024]{1,0:T(8,128)(2,1)S(1)}, bf16[256,1024]{1,0:T(8,128)(2,1)}, u32[]{:S(2)}) copy-start(bf16[256,1024]{1,0:T(8,128)(2,1)} %copy-done.9) | copy-start | bytes 1572868
  404.3 213.9 %reduce-scatter.27.cloned.1.call-start = ((), (), s32[]{:S(2)}) async-start(), calls=%async_computation.21 | async-start | bytes 589824
  414.3 271.1 %reduce-scatter.25.cloned.1.call-start = ((), (), s32[]{:S(2)}) async-start(), calls=%async_computation.20 | async-start | bytes 1769472
  433.1 1.0 copy-start.14
  433.1 1.8 copy-start.5
  433.2 2.5 copy-start.7
  435.6 0.8 copy-start.15
  435.8 1.3 copy-start.6
  435.8 2.0 copy-start.8
  454.2 1.1 copy-start.14
  454.2 1.8 copy-start.5
  454.2 2.4 copy-start.7
  456.7 0.8 copy-start.15
  456.9 1.3 copy-start.6
  456.9 2.0 copy-start.8
  459.1 4.2 copy-start.16
  470.7 247.5 %reduce-scatter.21.cloned.1.call-start = ((), (), s32[]{:S(2)}) async-start(), calls=%async_computation.18 | async-start | bytes 2621440 | tf_op jit(solution)/shard_map/reduce_scatter | solution.py:237
  475.4 79.9 %copy-start.19 = (f32[1024]{0:T(1024)S(1)}, f32[1024]{0:T(1024)}, u32[]{:S(2)}) copy-start(f32[1024]{0:T(1024)} %get-tuple-element.344) | copy-start | bytes 12292
  475.4 80.3 %copy-start.17 = (f32[1024]{0:T(1024)S(1)}, f32[1024]{0:T(1024)}, u32[]{:S(2)}) copy-start(f32[1024]{0:T(1024)} %get-tuple-element.348) | copy-start | bytes 12292
  475.4 80.3 %copy-start.18 = (f32[1024]{0:T(1024)S(1)}, f32[1024]{0:T(1024)}, u32[]{:S(2)}) copy-start(f32[1024]{0:T(1024)} %get-tuple-element.392) | copy-start | bytes 12292
  475.4 242.9 %copy-start.2 = (f32[256,1024]{1,0:T(8,128)S(1)}, f32[256,1024]{1,0:T(8,128)}, u32[]{:S(2)}) copy-start(f32[256,1024]{1,0:T(8,128)} %get-tuple-element.397) | copy-start | bytes 3145732
Sparse Core Ops, SparseCore 0:
  10.2 48.8 all-gather.9
  60.7 21.3 all-gather.7
  114.7 31.4 reduce-scatter.14
  148.3 49.2 all-gather.13
  199.7 21.0 all-gather.11
  222.9 51.0 all-gather.15
  280.2 29.6 reduce-scatter.16
  315.3 22.5 all-gather.17
  351.6 31.4 reduce-scatter.18
  388.3 22.5 all-gather.19
  414.9 68.1 reduce-scatter.28
  486.8 66.6 reduce-scatter.22
  557.2 60.9 reduce-scatter.26
  621.5 63.8 reduce-scatter.24
  687.9 30.3 reduce-scatter.20
where the time goes:
time: 735 us; the launch traced here: 727 us
  waiting for transfers between devices  463 us (63%)
  matrix products  91.6 us (12%)
  blocking collectives  72.2 us (10%)
  other arithmetic  37.3 us (5%)
  local copies, waits for them, and re-layouts  30.4 us (4%)
  loops' own time  16.3 us (2%)
  between operations  14.8 us (2%)
    reduce_scatter x4, waiting for transfers between devices, scatter_sum(): lax.psum_scatter(partial_sum.astype(jnp.bfloat16), axis_name, scatter_dim...  161 us
    unnamed x18, waiting for transfers between devices  96.9 us
    all_gather x1, waiting for transfers between devices, per_device(): lax.all_gather(up_weight, 'dp', axis=0, tiled=True)  44.8 us
    psum x1, blocking collectives, per_device(): lax.psum((gain_terms, bias_terms, hidden_terms), ('dp', 'tensor'))  41 us
    all_gather x1, waiting for transfers between devices, per_device(): lax.all_gather(down_weight, 'dp', axis=1, tiled=True)  38.3 us
    all_gather x1, blocking collectives, per_device(): lax.all_gather(output_weight, 'dp', axis=1, tiled=True)  31.2 us
    reduce_scatter x1, waiting for transfers between devices, per_device(): lax.psum_scatter(jnp.einsum('tc,ec->te', grad_matrix, back_triple, prefer...  30.9 us
    all_gather x1, waiting for transfers between devices, per_device(): lax.all_gather(first_out.astype(jnp.bfloat16), 'tensor', axis=0, tiled=True)  23.2 us
  transfers between devices with their start and end apart: 15, of which 15 were waited for; matrix products, arithmetic and copies ran while one was open for 13% of the time, Pallas kernels for 0%

commit v1 on v0

--- a/solution.py
+++ b/solution.py
@@ -274,7 +274,7 @@
         jnp.sum(grad_upper, axis=0, dtype=jnp.float32), tensor_rank, hidden_bias.shape[0]
     )
     grad_gains, grad_bias_rows, grad_hidden_bias = lax.psum(
-        (gain_terms, bias_terms, hidden_terms), ("dp", "tensor")
+        lax.psum((gain_terms, bias_terms, hidden_terms), "tensor"), "dp"
     )
     return (
         layer_out.astype(jnp.bfloat16),

time: 735 us -> 735 us (level)
    psum x1 -> x2, blocking collectives: 41 us -> 46.7 us  [the longest x1 36 us: per_device(): lax.psum(lax.psum((gain_terms, bias_terms, hidden_terms), 'tensor'), 'dp')]
where the time goes in v1:
time: 735 us; the launch traced here: 728 us
  waiting for transfers between devices  458 us (62%)
  matrix products  91.6 us (12%)
  blocking collectives  77.9 us (11%)
  other arithmetic  37.3 us (5%)
  local copies, waits for them, and re-layouts  30.4 us (4%)
  loops' own time  16.3 us (2%)
  between operations  14.8 us (2%)
    reduce_scatter x4, waiting for transfers between devices, scatter_sum(): lax.psum_scatter(partial_sum.astype(jnp.bfloat16), axis_name, scatter_dim...  161 us
    unnamed x18, waiting for transfers between devices  91.2 us
    all_gather x1, waiting for transfers between devices, per_device(): lax.all_gather(up_weight, 'dp', axis=0, tiled=True)  44.8 us
    all_gather x1, waiting for transfers between devices, per_device(): lax.all_gather(down_weight, 'dp', axis=1, tiled=True)  38.3 us
    psum x1, blocking collectives, per_device(): lax.psum(lax.psum((gain_terms, bias_terms, hidden_terms), 'tensor'), 'dp')  36 us
    all_gather x1, blocking collectives, per_device(): lax.all_gather(output_weight, 'dp', axis=1, tiled=True)  31.2 us
    reduce_scatter x1, waiting for transfers between devices, per_device(): lax.psum_scatter(jnp.einsum('tc,ec->te', grad_matrix, back_triple, prefer...  30.9 us
    all_gather x1, waiting for transfers between devices, per_device(): lax.all_gather(first_out.astype(jnp.bfloat16), 'tensor', axis=0, tiled=True)  23.2 us
  transfers between devices with their start and end apart: 15, of which 15 were waited for; matrix products, arithmetic and copies ran while one was open for 13% of the time, Pallas kernels for 0%

profile of v1, /device:TPU:0, one launch (start us, length us, event | category | flops | bytes accessed | tf_op | source)
XLA Modules:
  0.0 727.5 jit_solution(10590033260880652438)
XLA Ops:
  9.6 31.2 %all_gather.30 = bf16[256,1024]{1,0:T(8,128)(2,1)S(1)} all-gather(bf16[256,128]{1,0:T(8,128)(2,1)} %param.18), channel_id=1, replica_groups=mesh['dp'=8,'tensor'=4] {'dp'}, dimensions={1}, use_global_device_ids=true | all-gather | bytes 589824 | tf_op jit(solution)/shard_map/all_gather | solution.py:78
  40.7 18.4 %all-gather.10.cloned.1.call-done = bf16[1024,3,256]{2,0,1:T(8,128)(2,1)} async-done(((bf16[128,3,256]{2,0,1:T(8,128)(2,1)}), bf16[1024,3,256]{2,0,1:T(8,128)(2,1)}) %all-gather.10.cloned.1.call-update) | async-done | bytes 1572880 | tf_op jit(solution)/shard_map/all_gather | solution.py:77
  60.8 21.3 %all-gather.8.cloned.1.call-done = bf16[1024,1024]{1,0:T(8,128)(2,1)} async-done(((bf16[256,1024]{1,0:T(8,128)(2,1)}), bf16[1024,1024]{1,0:T(8,128)(2,1)}) %all-gather.8.cloned.1.call-update) | async-done | bytes 2097168 | tf_op jit(solution)/shard_map/all_gather | solution.py:84
  82.1 3.4 fusion.20
  89.6 22.9 %while.30 = (s32[]{:T(128)}, bf16[2,512,256]{2,1,0:T(8,128)(2,1)S(1)}, f32[2,4,512]{2,1,0:T(4,128)S(1)}, s32[2]{0:T(128)S(1)}, s32[1,1024]{1,0:T(1,128)S(1)}, /*...) while((s32[]{:T(128)}, ...), condition=%wide.region_3.4_spmd, body=%wide.region_0.3_spmd.sunk | while | flops 562690048 | bytes 30484896 | solution.py:121
  95.6 2.3 fusion.103
  97.9 2.9 fusion.104
  107.0 2.3 fusion.103
  109.3 2.9 fusion.104
  115.2 30.9 %reduce-scatter.15.cloned.1.call-done = bf16[256,1024]{1,0:T(8,128)(2,1)} async-done(((bf16[1024,1024]{1,0:T(8,128)(2,1)}), bf16[256,1024]{1,0:T(8,128)(2,1)}) %reduce-scatter.15.cloned.1.call-update) | async-done | bytes 524304 | tf_op jit(solution)/shard_map/reduce_scatter | solution.py:42
  148.8 2.1 fusion.37
  152.8 44.8 %all-gather.14.cloned.1.call-done = bf16[1024,1024]{1,0:T(8,128)(2,1)} async-done(((bf16[128,1024]{1,0:T(8,128)(2,1)}), bf16[1024,1024]{1,0:T(8,128)(2,1)}) %all-gather.14.cloned.1.call-update) | async-done | bytes 2097168 | tf_op jit(solution)/shard_map/all_gather | solution.py:79
  197.7 23.2 %all-gather.12.cloned.1.call-done = bf16[1024,1024]{1,0:T(8,128)(2,1)} async-done(((bf16[256,1024]{1,0:T(8,128)(2,1)}), bf16[1024,1024]{1,0:T(8,128)(2,1)}) %all-gather.12.cloned.1.call-update) | async-done | bytes 2097168 | tf_op jit(solution)/shard_map/all_gather | solution.py:132
  220.8 14.9 %multiply_convert_fusion.1 = (bf16[1024,1024]{1,0:T(8,128)(2,1)}, f32[1024,1024]{1,0:T(8,128)}, f32[1024,1024]{1,0:T(8,128)}) fusion(f32[1024]{0:T(1024)S(1)} %dynamic_slice.57, bf16[1024,1024]{1,0:T(8,128)(2,1)} %all-gather.12.cloned.1.call-done, bf16[1024,1024]{1,0:T(8,128)(2,1)} %all-gather.14.cloned.1.call-done), kind=kOutput, calls=%fused_computation.37 | convolution fusion | flops 2216689664 | bytes 14684160 | tf_op jit(solution)/shard_map/dot_general | solution.py:135
  235.7 38.3 %all-gather.16.cloned.1.call-done = bf16[1024,1024]{1,0:T(8,128)(2,1)} async-done(((bf16[1024,128]{1,0:T(8,128)(2,1)}), bf16[1024,1024]{1,0:T(8,128)(2,1)}) %all-gather.16.cloned.1.call-update) | async-done | bytes 2097168 | tf_op jit(solution)/shard_map/all_gather | solution.py:80
  274.0 6.0 convolution_convert_fusion.3
  280.1 29.7 %reduce-scatter.17.cloned.1.call-done = bf16[256,1024]{1,0:T(8,128)(2,1)} async-done(((bf16[1024,1024]{1,0:T(8,128)(2,1)}), bf16[256,1024]{1,0:T(8,128)(2,1)}) %reduce-scatter.17.cloned.1.call-update) | async-done | bytes 524304 | tf_op jit(solution)/shard_map/reduce_scatter | solution.py:42
  312.7 2.4 convert_reduce_fusion.2
  315.4 22.5 %all-gather.18.cloned.1.call-done = bf16[1024,1024]{1,0:T(8,128)(2,1)} async-done(((bf16[256,1024]{1,0:T(8,128)(2,1)}), bf16[1024,1024]{1,0:T(8,128)(2,1)}) %all-gather.18.cloned.1.call-update) | async-done | bytes 2097168 | tf_op jit(solution)/shard_map/all_gather | solution.py:159
  337.9 8.5 %convert_reduce_fusion = (f32[1024]{0:T(1024)S(1)}, bf16[1024,1024]{1,0:T(8,128)(2,1)S(1)}) fusion(f32[1024,1024]{1,0:T(8,128)} %get-tuple-element.404, f32[1024,1024]{1,0:T(8,128)} %get-tuple-element.422, f32[1024]{0:T(1024)S(1)} %dynamic_slice.57, bf16[1024,1024]{1,0:T(8,128)(2,1)} %all-gather.18.cloned.1.call-done, ...), kind=kOutput, calls=%fused_computation.35 | convolution fusion | flops 2165308416 | bytes 14688256 | tf_op jit(solution)/shard_map/td,fd->tf/dot_general | solution.py:163
  347.7 3.7 convolution_convert_fusion.2
  351.5 31.6 %reduce-scatter.19.cloned.1.call-done = bf16[256,1024]{1,0:T(8,128)(2,1)} async-done(((bf16[1024,1024]{1,0:T(8,128)(2,1)}), bf16[256,1024]{1,0:T(8,128)(2,1)}) %reduce-scatter.19.cloned.1.call-update) | async-done | bytes 524304 | tf_op jit(solution)/shard_map/reduce_scatter | solution.py:42
  383.1 2.0 multiply_reduce_fusion.1
  385.1 3.0 convert_reduce_fusion.3
  388.2 5.9 convolution_convert_fusion
  394.1 4.1 copy.60
  398.3 6.0 convolution_convert_fusion.1
  404.5 6.4 all-gather.20.cloned.1.call-done
  410.9 2.3 convolution_convert_fusion.5
  414.3 2.3 convolution_convert_fusion.6
  416.7 42.4 %while.31 = (s32[]{:T(128)}, bf16[2,512,256]{1,2,0:T(8,128)(2,1)}, f32[2,1024,256]{1,2,0:T(8,128)}, f32[2,1024,256]{1,2,0:T(8,128)}, s32[2]{0:T(128)S(1)}, /*ind...) while((s32[]{:T(128)}, bf16[2,512,256]{1,2,0:T(8,128)(2,1)}, ...), condition=%wide.region_17.18_spmd, body=%wide.region_15.17_spmd.sunk | while | flops 1374681088 | bytes 114100872 | solution.py:219
  423.8 2.4 fusion.116
  426.2 3.2 multiply_reduce_fusion.7
  429.4 2.4 multiply_convert_fusion.3
  444.9 2.4 fusion.116
  447.3 3.2 multiply_reduce_fusion.7
  450.4 2.4 multiply_convert_fusion.3
  463.5 4.6 fusion.22
  468.1 2.6 copy.62
  470.8 4.6 bitcast_convert_fusion
  475.7 7.3 %reduce-scatter.29.cloned.1.call-done = bf16[128,1024]{1,0:T(8,128)(2,1)} async-done(((bf16[1024,1024]{1,0:T(8,128)(2,1)}), bf16[128,1024]{1,0:T(8,128)(2,1)}) %reduce-scatter.29.cloned.1.call-update) | async-done | bytes 262160
  485.0 68.5 %reduce-scatter.23.cloned.1.call-done = bf16[128,1024]{1,0:T(8,128)(2,1)} async-done(((bf16[1024,1024]{1,0:T(8,128)(2,1)}), bf16[128,1024]{1,0:T(8,128)(2,1)}) %reduce-scatter.23.cloned.1.call-update) | async-done | bytes 262160 | tf_op jit(solution)/shard_map/reduce_scatter | solution.py:42
  555.7 10.7 %all-reduce.1 = (f32[2,1024]{1,0:T(2,128)S(1)}, f32[6,1024]{1,0:T(8,128)S(1)}, f32[4096]{0:T(1024)S(1)}) all-reduce(f32[2,1024]{1,0:T(2,128)S(1)} %pad_maximum_fusion.3, f32[6,1024]{1,0:T(8,128)S(1)} %concatenate.3, f32[4096]{0:T(1024)S(1)} %dynamic_update_slice.41), channel_id=1, replica_groups=mesh['dp'=8,'tensor'=4] {'tensor'}, use_global_device_ids=true, to_apply=%region_27.28 | all-reduce | flops 12288 | bytes 98304 | tf_op jit(solution)/shard_map/psum | solution.py:277
  566.5 36.0 %all-reduce = (f32[2,1024]{1,0:T(2,128)}, f32[6,1024]{1,0:T(8,128)}, f32[4096]{0:T(1024)}) all-reduce(f32[2,1024]{1,0:T(2,128)S(1)} %get-tuple-element.390, f32[6,1024]{1,0:T(8,128)S(1)} %get-tuple-element.391, f32[4096]{0:T(1024)S(1)} %get-tuple-element.392), channel_id=1, replica_groups=mesh['dp'=8,'tensor'=4] {'dp'}, use_global_device_ids=true, to_apply=%region_28.29 | all-reduce | flops 12288 | bytes 98304 | tf_op jit(solution)/shard_map/psum | solution.py:276
  602.5 15.7 %reduce-scatter.27.cloned.1.call-done = bf16[128,256]{1,0:T(8,128)(2,1)} async-done(((bf16[1024,256]{1,0:T(8,128)(2,1)}), bf16[128,256]{1,0:T(8,128)(2,1)}) %reduce-scatter.27.cloned.1.call-update) | async-done | bytes 65552
  619.8 65.6 %reduce-scatter.25.cloned.1.call-done = bf16[128,768]{1,0:T(8,128)(2,1)} async-done(((bf16[1024,768]{1,0:T(8,128)(2,1)}), bf16[128,768]{1,0:T(8,128)(2,1)}) %reduce-scatter.25.cloned.1.call-update) | async-done | bytes 196624
  687.4 30.9 %reduce-scatter.21.cloned.1.call-done = bf16[256,1024]{1,0:T(8,128)(2,1)} async-done(((bf16[1024,1024]{1,0:T(8,128)(2,1)}), bf16[256,1024]{1,0:T(8,128)(2,1)}) %reduce-scatter.21.cloned.1.call-update) | async-done | bytes 524304 | tf_op jit(solution)/shard_map/reduce_scatter | solution.py:237
  718.3 2.2 convert_add_fusion
  (181 shorter events, 56.5 us)
Async XLA Ops:
  7.2 51.9 %all-gather.10.cloned.1.call-start = ((), (), s32[]{:S(2)}) async-start(), calls=%async_computation.9 | async-start | bytes 1769472 | tf_op jit(solution)/shard_map/all_gather | solution.py:77
  7.9 74.2 %all-gather.8.cloned.1.call-start = ((), (), s32[]{:S(2)}) async-start(), calls=%async_computation.8 | async-start | bytes 2621440 | tf_op jit(solution)/shard_map/all_gather | solution.py:84
  8.7 137.5 %reduce-scatter.15.cloned.1.call-start = ((), (), s32[]{:S(2)}) async-start(), calls=%async_computation.10 | async-start | bytes 2621440 | tf_op jit(solution)/shard_map/reduce_scatter | solution.py:42
  40.7 71.8 %copy-start.9 = (bf16[256,1024]{1,0:T(8,128)(2,1)}, bf16[256,1024]{1,0:T(8,128)(2,1)S(1)}, u32[]{:S(2)}) copy-start(bf16[256,1024]{1,0:T(8,128)(2,1)S(1)} %all_gather.30) | copy-start | bytes 1572868
  85.5 1.7 copy-start.3
  87.2 2.4 copy-start.13
  112.5 38.5 %copy-start.11 = (bf16[2,512,256]{2,1,0:T(8,128)(2,1)}, bf16[2,512,256]{2,1,0:T(8,128)(2,1)S(1)}, u32[]{:S(2)}) copy-start(bf16[2,512,256]{2,1,0:T(8,128)(2,1)S(1)} %get-tuple-element.252) | copy-start | bytes 1572868
  112.5 2.7 copy-start.21
  112.5 2.7 copy-start.20
  112.5 33.6 %copy-start = (bf16[256,1024]{1,0:T(8,128)(2,1)S(1)}, bf16[256,1024]{1,0:T(8,128)(2,1)}, u32[]{:S(2)}) copy-start(bf16[256,1024]{1,0:T(8,128)(2,1)} %param.14) | copy-start | bytes 1572868
  114.6 83.1 %all-gather.14.cloned.1.call-start = ((), (), s32[]{:S(2)}) async-start(), calls=%async_computation.12 | async-start | bytes 2359296 | tf_op jit(solution)/shard_map/all_gather | solution.py:79
  115.1 105.7 %all-gather.12.cloned.1.call-start = ((), (), s32[]{:S(2)}) async-start(), calls=%async_computation.11 | async-start | bytes 2621440 | tf_op jit(solution)/shard_map/all_gather | solution.py:132
  151.0 123.1 %all-gather.16.cloned.1.call-start = ((), (), s32[]{:S(2)}) async-start(), calls=%async_computation.13 | async-start | bytes 2359296 | tf_op jit(solution)/shard_map/all_gather | solution.py:80
  151.6 158.2 %reduce-scatter.17.cloned.1.call-start = ((), (), s32[]{:S(2)}) async-start(), calls=%async_computation.14 | async-start | bytes 2621440 | tf_op jit(solution)/shard_map/reduce_scatter | solution.py:42
  274.0 35.8 %copy-start.1 = (bf16[256,1024]{1,0:T(8,128)(2,1)S(1)}, bf16[256,1024]{1,0:T(8,128)(2,1)}, u32[]{:S(2)}) copy-start(bf16[256,1024]{1,0:T(8,128)(2,1)} %reduce-scatter.15.cloned.1.call-done) | copy-start | bytes 1572868
  280.0 31.6 %copy-start.4 = (bf16[256,1024]{1,0:T(8,128)(2,1)S(1)}, bf16[256,1024]{1,0:T(8,128)(2,1)}, u32[]{:S(2)}) copy-start(bf16[256,1024]{1,0:T(8,128)(2,1)} %param.16) | copy-start | bytes 1572868
  280.0 57.9 %all-gather.18.cloned.1.call-start = ((), (), s32[]{:S(2)}) async-start(), calls=%async_computation.15 | async-start | bytes 2621440 | tf_op jit(solution)/shard_map/all_gather | solution.py:159
  315.2 67.9 %reduce-scatter.19.cloned.1.call-start = ((), (), s32[]{:S(2)}) async-start(), calls=%async_computation.16 | async-start | bytes 2621440 | tf_op jit(solution)/shard_map/reduce_scatter | solution.py:42
  337.9 9.8 %copy-start.22 = (bf16[1024,1024]{1,0:T(8,128)(2,1)S(1)}, bf16[1024,1024]{1,0:T(8,128)(2,1)}, u32[]{:S(2)}) copy-start(bf16[1024,1024]{1,0:T(8,128)(2,1)} %all-gather.14.cloned.1.call-done) | copy-start | bytes 6291460
  346.4 1.3 copy-start.23
  351.5 59.4 %all-gather.20.cloned.1.call-start = ((), (), s32[]{:S(2)}) async-start(), calls=%async_computation.17 | async-start | bytes 2621440 | tf_op jit(solution)/shard_map/all_gather | solution.py:180
  388.2 94.9 %reduce-scatter.29.cloned.1.call-start = ((), (), s32[]{:S(2)}) async-start(), calls=%async_computation.22 | async-start | bytes 2359296
  398.2 12.7 %copy-start.12 = (bf16[2,512,256]{2,1,0:T(8,128)(2,1)S(1)}, bf16[2,512,256]{2,1,0:T(8,128)(2,1)}, u32[]{:S(2)}) copy-start(bf16[2,512,256]{2,1,0:T(8,128)(2,1)} %copy-done.11) | copy-start | bytes 1572868
  398.2 155.3 %reduce-scatter.23.cloned.1.call-start = ((), (), s32[]{:S(2)}) async-start(), calls=%async_computation.19 | async-start | bytes 2359296 | tf_op jit(solution)/shard_map/reduce_scatter | solution.py:42
  404.2 10.1 %copy-start.10 = (bf16[256,1024]{1,0:T(8,128)(2,1)S(1)}, bf16[256,1024]{1,0:T(8,128)(2,1)}, u32[]{:S(2)}) copy-start(bf16[256,1024]{1,0:T(8,128)(2,1)} %copy-done.9) | copy-start | bytes 1572868
  404.3 214.0 %reduce-scatter.27.cloned.1.call-start = ((), (), s32[]{:S(2)}) async-start(), calls=%async_computation.21 | async-start | bytes 589824
  414.3 271.1 %reduce-scatter.25.cloned.1.call-start = ((), (), s32[]{:S(2)}) async-start(), calls=%async_computation.20 | async-start | bytes 1769472
  433.1 1.0 copy-start.14
  433.1 1.8 copy-start.5
  433.2 2.5 copy-start.7
  435.6 0.8 copy-start.15
  435.8 1.3 copy-start.6
  435.8 2.0 copy-start.8
  454.2 1.1 copy-start.14
  454.2 1.8 copy-start.5
  454.2 2.4 copy-start.7
  456.7 0.8 copy-start.15
  456.9 1.3 copy-start.6
  456.9 2.0 copy-start.8
  459.1 4.2 copy-start.16
  470.7 247.6 %reduce-scatter.21.cloned.1.call-start = ((), (), s32[]{:S(2)}) async-start(), calls=%async_computation.18 | async-start | bytes 2621440 | tf_op jit(solution)/shard_map/reduce_scatter | solution.py:237
  475.4 79.9 %copy-start.19 = (f32[1024]{0:T(1024)S(1)}, f32[1024]{0:T(1024)}, u32[]{:S(2)}) copy-start(f32[1024]{0:T(1024)} %get-tuple-element.344) | copy-start | bytes 12292
  475.4 80.3 %copy-start.17 = (f32[1024]{0:T(1024)S(1)}, f32[1024]{0:T(1024)}, u32[]{:S(2)}) copy-start(f32[1024]{0:T(1024)} %get-tuple-element.348) | copy-start | bytes 12292
  475.4 80.3 %copy-start.18 = (f32[1024]{0:T(1024)S(1)}, f32[1024]{0:T(1024)}, u32[]{:S(2)}) copy-start(f32[1024]{0:T(1024)} %get-tuple-element.395) | copy-start | bytes 12292
  475.4 243.0 %copy-start.2 = (f32[256,1024]{1,0:T(8,128)S(1)}, f32[256,1024]{1,0:T(8,128)}, u32[]{:S(2)}) copy-start(f32[256,1024]{1,0:T(8,128)} %get-tuple-element.400) | copy-start | bytes 3145732
Sparse Core Ops, SparseCore 0:
  10.2 48.8 all-gather.9
  60.7 21.3 all-gather.7
  114.7 31.4 reduce-scatter.14
  148.3 49.2 all-gather.13
  199.7 21.0 all-gather.11
  222.9 51.0 all-gather.15
  280.2 29.6 reduce-scatter.16
  315.3 22.5 all-gather.17
  351.6 31.4 reduce-scatter.18
  388.3 22.5 all-gather.19
  414.9 68.1 reduce-scatter.28
  486.8 66.6 reduce-scatter.22
  557.2 60.9 reduce-scatter.26
  621.5 63.8 reduce-scatter.24
  687.9 30.3 reduce-scatter.20
